TPU v7x, 256 devices: a whole 4x4x8 slice. The times are simulated.
256 devices in a mesh: comp: 4 (over y), gx: 8 (over x, z_lo), gy: 8 (over z_hi, core).
Axes of the slice: x: 4, y: 4, z: 8 (z_hi: 4, z_lo: 2; z = z_hi * 2 + z_lo), core: 2. Of those that a mesh axis runs over, the one named last changes fastest.
Arguments:
- zonal_flow_speed: float32 [64, 128, 1024], P('comp', 'gx', 'gy'), may hold values from -5 to 5
- meridional_flow_speed: float32 [64, 128, 1024], P('comp', 'gx', 'gy'), may hold values from -5 to 5
- thermal_anomaly: float32 [64, 128, 1024], P('comp', 'gx', 'gy'), may hold values from -6 to 6
- brine_anomaly_values: float32 [64, 128, 1024], P('comp', 'gx', 'gy'), may hold values from -6 to 6
- marine_indicator: int32 [128, 1024], P('gx', 'gy'), may hold values 0 or 1
- seafloor_layer: int32 [128, 1024], P('gx', 'gy'), may hold values from 1 to 64
- dissolved_species: float32 [24, 64, 8, 4, 4, 1024], P(None, None, 'gx', 'comp', None, 'gy'), may hold values from 0.05 to 2
- topmost_sunshine: float32 [8, 4, 4, 1024], P('gx', 'comp', None, 'gy'), may hold values from 0.3 to 3
- attenuation_coefficient: float32 [24], replicated, may hold values from 0.01 to 0.1
- peak_intake_speed: float32 [24], replicated, may hold values from 0.2 to 2
- feedstock_midpoint_constant: float32 [24], replicated, may hold values from 0.05 to 1
- photon_midpoint_constant: float32 [24], replicated, may hold values from 0.05 to 1
- stoichiometry_matrix: float32 [24, 24], replicated, may hold values from -1.25 to 1.25
Outputs:
- east_new: float32 [64, 128, 1024], P('comp', 'gx', 'gy')
- north_new: float32 [64, 128, 1024], P('comp', 'gx', 'gy')
- warmed_result: float32 [64, 128, 1024], P('comp', 'gx', 'gy')
- salt_mixed: float32 [64, 128, 1024], P('comp', 'gx', 'gy')
- buoyancy: float32 [64, 128, 1024], P('comp', 'gx', 'gy')
- result: float32 [24, 64, 8, 4, 4, 1024], P(None, None, 'gx', 'comp', None, 'gy')
All inputs are finite; a program needn't handle non-finite values. No bound on the sum of `marine_indicator` on one device may be relied on, other than what follows from the above.
Results may differ from a plain program's by a relative error of at most 0.00007.
Values sent between devices are 32-bit elements; how exact they have to be, the bound alone decides.
A program may use at most 128 MiB of HBM per device.

v0:
```python
import jax
import jax.numpy as jnp
from jax import lax
from jax.sharding import PartitionSpec as P

NSUB = 2
DT_FLOW = 0.1
CORIOLIS = 0.3
MIXING = 0.15
COURANT = 0.24
DT_BIO = 0.5
WARMING_FACTOR = 0.5
CLEAR_WATER = 0.5
HIGHEST = lax.Precision.HIGHEST


def padded(x, sides, width):
    edges = {}
    for axis, dim in sides:
        count, length = (lax.axis_size(axis), x.shape[dim])
        up = [(i, (i + 1) % count) for i in range(count - 1)]
        last = lax.slice_in_dim(x, length - width, length, axis=dim)
        first = lax.slice_in_dim(x, 0, width, axis=dim)
        edges[dim] = (
            lax.ppermute(last, axis, up),
            lax.ppermute(first, axis, [(b, a) for a, b in up]),
        )
    done = []
    for _, dim in sides:
        low, high = edges[dim]
        around = [(width, width) if d in done else (0, 0) for d in range(x.ndim)]
        x = jnp.concatenate([jnp.pad(low, around), x, jnp.pad(high, around)], axis=dim)
        done.append(dim)
    return x


def from_everyone(x, axis):
    copies = jnp.broadcast_to(x, (lax.axis_size(axis), *x.shape))
    return lax.all_to_all(copies, axis, split_axis=0, concat_axis=0, tiled=True)


def in_order(pieces, dim):
    dims = list(pieces.shape[1:])
    dims[dim] *= pieces.shape[0]
    return jnp.moveaxis(pieces, 0, dim).reshape(dims)


def collect(x, axis, dim):
    pieces = from_everyone(x, axis)
    return in_order(pieces, dim)


def from_behind(x, axis, by):
    count = lax.axis_size(axis)
    pairs = [(i, i + by) for i in range(count) if 0 <= i + by < count]
    return lax.ppermute(x, axis, pairs)


def passed_along(x, axis, by):
    count = lax.axis_size(axis)
    return lax.ppermute(x, axis, [(i, (i + by) % count) for i in range(count)])


def extended_2(cells, sides, width):
    for axis, dim in sides:
        count = lax.axis_size(axis)
        ends = count - 1
        head = lax.slice_in_dim(cells, 0, width, axis=dim)
        tail = lax.slice_in_dim(cells, cells.shape[dim] - width, cells.shape[dim], axis=dim)
        cells = jnp.concatenate(
            [
                lax.ppermute(tail, axis, [(i, (i + 1) % count) for i in range(ends)]),
                cells,
                lax.ppermute(head, axis, [((i + 1) % count, i) for i in range(ends)]),
            ],
            axis=dim,
        )
    return cells


def on_device(
    zonal_flow_speed,
    meridional_flow_speed,
    thermal_anomaly,
    brine_anomaly_values,
    marine_indicator,
    seafloor_layer,
    dissolved_species,
    topmost_sunshine,
    attenuation_coefficient,
    peak_intake_speed,
    feedstock_midpoint_constant,
    photon_midpoint_constant,
    stoichiometry_matrix,
):
    group_index = lax.axis_index("comp")
    group_count = lax.axis_size("comp")
    levels_dev, tile_rows, tile_cols = zonal_flow_speed.shape
    tracer_count = dissolved_species.shape[0]
    level_count = dissolved_species.shape[1]
    sub_rows = dissolved_species.shape[4]
    rimmed = padded(jnp.stack([marine_indicator, seafloor_layer]), (("gx", 1), ("gy", 2)), 1)
    depth_index = group_index * levels_dev + jnp.arange(levels_dev, dtype=jnp.int32)[:, None, None]
    wet_rimmed = ((rimmed[0][None] == 1) & (depth_index < rimmed[1][None])).astype(jnp.float32)
    submerged_indicator = wet_rimmed[:, 1:-1, 1:-1]
    face_east = wet_rimmed[:, :-1, 1:-1] * wet_rimmed[:, 1:, 1:-1]
    face_north = wet_rimmed[:, 1:-1, :-1] * wet_rimmed[:, 1:-1, 1:]
    open_east = face_east[:, 1:]
    open_north = face_north[:, :, 1:]
    seawater_heaviness = submerged_indicator * (-0.2 * thermal_anomaly + 0.8 * brine_anomaly_values)
    column_total = jnp.sum(seawater_heaviness, axis=0)
    totals = collect(column_total[None], "comp", 0)
    earlier_groups = (jnp.arange(group_count, dtype=jnp.int32) < group_index).astype(jnp.float32)
    offset = jnp.sum(totals * earlier_groups[:, None, None], axis=0)
    strict_lower = (jnp.arange(levels_dev)[:, None] > jnp.arange(levels_dev)[None, :]).astype(
        jnp.float32
    )
    depth_above = offset[None] + jnp.dot(
        strict_lower, seawater_heaviness.reshape(levels_dev, -1), precision=HIGHEST
    ).reshape(seawater_heaviness.shape)
    weight_of_overlying = depth_above + 0.5 * seawater_heaviness
    padded_field = padded(
        jnp.stack([thermal_anomaly, brine_anomaly_values, weight_of_overlying]),
        (("gx", 2), ("gy", 3)),
        1,
    )
    pressure_east = padded_field[2, :, 2:, 1:-1]
    pressure_north = padded_field[2, :, 1:-1, 2:]
    east_new = open_east * (
        zonal_flow_speed
        + DT_FLOW * (CORIOLIS * meridional_flow_speed - (pressure_east - weight_of_overlying))
    )
    north_new = open_north * (
        meridional_flow_speed
        + DT_FLOW * (-CORIOLIS * zonal_flow_speed - (pressure_north - weight_of_overlying))
    )
    east_column, north_column = (
        lax.all_to_all(east_new, "comp", split_axis=1, concat_axis=0, tiled=True),
        lax.all_to_all(north_new, "comp", split_axis=1, concat_axis=0, tiled=True),
    )
    scalar_pair = padded_field[:2]
    flux_east = face_east[None] * (scalar_pair[:, :, 1:, 1:-1] - scalar_pair[:, :, :-1, 1:-1])
    flux_north = face_north[None] * (scalar_pair[:, :, 1:-1, 1:] - scalar_pair[:, :, 1:-1, :-1])
    blended_couple = scalar_pair[:, :, 1:-1, 1:-1] + MIXING * (
        flux_east[:, :, 1:]
        - flux_east[:, :, :-1]
        + (flux_north[:, :, :, 1:] - flux_north[:, :, :, :-1])
    )
    thermal_blended = blended_couple[0]
    salt_mixed = blended_couple[1]
    courant_east = COURANT * jnp.tanh(east_column)
    courant_north = COURANT * jnp.tanh(north_column)
    row_start = group_index * sub_rows
    sea_rows = lax.dynamic_slice_in_dim(marine_indicator, row_start, sub_rows, 0)
    bottom_rows = lax.dynamic_slice_in_dim(seafloor_layer, row_start, sub_rows, 0)
    column_depth = jnp.arange(level_count, dtype=jnp.int32)[:, None, None]
    wet_column = ((sea_rows[None] == 1) & (column_depth < bottom_rows[None])).astype(jnp.float32)
    north_before = from_behind(courant_north[:, :, -1], "gy", 1)
    courant_faces = jnp.concatenate([north_before[:, :, None], courant_north], axis=2)

    def neighbour_row(edge_row, shift_by, edge_group):
        within = passed_along(edge_row, "comp", shift_by)
        across = from_behind(within, "gx", shift_by)
        return jnp.where(group_index == edge_group, across, within)

    tracer_field = dissolved_species.reshape(tracer_count, level_count, sub_rows, tile_cols)
    east_below = neighbour_row(courant_east[:, -1], 1, 0)
    east_faces = jnp.concatenate([east_below[:, None], courant_east], axis=1)
    for substep in range(NSUB):
        row_below = neighbour_row(tracer_field[:, :, -1], 1, 0)
        beyond = neighbour_row(tracer_field[:, :, 0], -1, group_count - 1)
        extended = jnp.concatenate(
            [row_below[:, :, None], tracer_field, beyond[:, :, None]], axis=2
        )
        flux_faces = (
            jnp.maximum(east_faces, 0.0) * extended[:, :, :-1]
            + jnp.minimum(east_faces, 0.0) * extended[:, :, 1:]
        )
        change_east = flux_faces[:, :, 1:] - flux_faces[:, :, :-1]
        north_field = extended_2(tracer_field, (("gy", 3),), 1)
        flux_column = (
            jnp.maximum(courant_faces, 0.0) * north_field[:, :, :, :-1]
            + jnp.minimum(courant_faces, 0.0) * north_field[:, :, :, 1:]
        )
        change_north = flux_column[:, :, :, 1:] - flux_column[:, :, :, :-1]
        tracer_field = wet_column * (tracer_field - change_east - change_north)
    layer_depth = 2.0 / level_count
    optical_step = layer_depth * (
        CLEAR_WATER
        + jnp.tensordot(attenuation_coefficient, tracer_field, axes=1, precision=HIGHEST)
    )
    strict_column = (jnp.arange(level_count)[:, None] > jnp.arange(level_count)[None, :]).astype(
        jnp.float32
    )
    optical_above = jnp.dot(
        strict_column, optical_step.reshape(level_count, -1), precision=HIGHEST
    ).reshape(optical_step.shape)
    transmitted = jnp.exp(-optical_above)
    surface = topmost_sunshine.reshape(sub_rows, tile_cols)[None]
    light_level = surface * transmitted * jnp.exp(-0.5 * optical_step)
    warming_step = wet_column * surface * transmitted * (1.0 - jnp.exp(-optical_step)) / layer_depth
    warming_reverse = lax.all_to_all(warming_step, "comp", split_axis=0, concat_axis=1, tiled=True)
    nutrient = tracer_field[0]
    uptake_rates = (
        peak_intake_speed[:, None, None, None]
        * (nutrient / (feedstock_midpoint_constant[:, None, None, None] + nutrient))
        * (light_level / (light_level + photon_midpoint_constant[:, None, None, None]))
        * tracer_field
    )
    change = jnp.tensordot(stoichiometry_matrix, uptake_rates, axes=1, precision=HIGHEST)
    result = tracer_field + DT_BIO * wet_column * change
    warmed_result = thermal_blended + WARMING_FACTOR * warming_reverse
    buoyancy = submerged_indicator * (0.2 * warmed_result - 0.8 * salt_mixed)
    return (
        east_new,
        north_new,
        warmed_result,
        salt_mixed,
        buoyancy,
        result.reshape(dissolved_species.shape),
    )


def solution(mesh):
    return jax.shard_map(
        on_device,
        mesh=mesh,
        in_specs=(
            P("comp", "gx", "gy"),
            P("comp", "gx", "gy"),
            P("comp", "gx", "gy"),
            P("comp", "gx", "gy"),
            P("gx", "gy"),
            P("gx", "gy"),
            P(None, None, "gx", "comp", None, "gy"),
            P("gx", "comp", None, "gy"),
            P(),
            P(),
            P(),
            P(),
            P(),
        ),
        out_specs=(
            P("comp", "gx", "gy"),
            P("comp", "gx", "gy"),
            P("comp", "gx", "gy"),
            P("comp", "gx", "gy"),
            P("comp", "gx", "gy"),
            P(None, None, "gx", "comp", None, "gy"),
        ),
        check_vma=False,
    )
```

profile of v0, /device:TPU:15, one launch (start us, length us, event | category | flops | bytes accessed | tf_op | source)
XLA Modules:
  0.0 252.4 jit_solution(14438228290551515185)
XLA Ops:
  1.5 2.6 %collective-permute-start.3 = (s32[2,16,1]{2,1,0:T(8,128)S(1)}, s32[2,16,1]{2,1,0:T(8,128)S(1)}, u32[]{:S(2)}, u32[]{:S(2)}) collective-permute-start(s32[2,16,1]{2,1,0:T(8,128)S(1)} %get-tuple-element.73), channel_id=1, source_target_pairs={{1,0},{2,1},{3,2},{4,3},{5,4},{6,5},{7,6},{9,8},{10,9},{11,10},{12... | collective-permute-start | bytes 392 | tf_op jit(solution)/shard_map/ppermute | solution.py:26
  4.1 4.8 %collective-permute-start = (s32[2,16,1]{2,1,0:T(8,128)S(1)}, s32[2,16,1]{2,1,0:T(8,128)S(1)}, u32[]{:S(2)}, u32[]{:S(2)}) collective-permute-start(s32[2,16,1]{2,1,0:T(8,128)S(1)} %get-tuple-element.72), channel_id=1, source_target_pairs={{0,1},{1,2},{2,3},{3,4},{4,5},{5,6},{6,7},{8,9},{9,10},{10,11},{11... | collective-permute-start | bytes 392 | tf_op jit(solution)/shard_map/ppermute | solution.py:25
  9.6 3.8 %collective-permute-start.2 = (s32[2,1,128]{2,1,0:T(1,128)S(1)}, s32[2,1,128]{2,1,0:T(1,128)S(1)}, u32[]{:S(2)}, u32[]{:S(2)}) collective-permute-start(s32[2,1,128]{2,1,0:T(1,128)S(1)} %get-tuple-element.71), channel_id=1, source_target_pairs={{8,0},{16,8},{24,16},{32,24},{40,32},{48,40},{56,48},{9,1},{17,9},... | collective-permute-start | bytes 3080 | tf_op jit(solution)/shard_map/ppermute | solution.py:26
  13.4 1.9 collective-permute-start.1
  15.4 3.7 %copy.347 = f32[24,64,1,1,4,128]{5,0,1,4,3,2:T(8,128)S(1)} copy(f32[24,64,1,1,4,128]{5,4,3,2,1,0:T(4,128)} %param.19) | data formatting | bytes 6291456 | tf_op args[6]
  19.1 3.6 %fusion.72 = (f32[24,64,4,1]{3,0,1,2:T(8,128)}, f32[24,64,4,1]{3,0,1,2:T(8,128)}) fusion(f32[24,64,4,128]{3,0,1,2:T(8,128)S(1)} %bitcast.166), kind=kLoop, calls=%fused_computation.157 | loop fusion | bytes 98304 | tf_op jit(solution)/shard_map/slice | solution.py:69
  22.7 3.1 %copy.252 = f32[24,64,4,1]{1,0,3,2:T(8,128)} copy(f32[24,64,4,1]{3,0,1,2:T(8,128)} %get-tuple-element.54) | data formatting | bytes 49152 | tf_op jit(solution)/shard_map/slice | solution.py:69
  25.8 2.7 %collective-permute-start.15 = (f32[24,64,4,1]{1,0,3,2:T(8,128)}, f32[24,64,4,1]{1,0,3,2:T(8,128)}, u32[]{:S(2)}, u32[]{:S(2)}) collective-permute-start(f32[24,64,4,1]{1,0,3,2:T(8,128)} %copy.252), channel_id=1, source_target_pairs={{0,1},{1,2},{2,3},{3,4},{4,5},{5,6},{6,7},{8,9},{9,10},{10,11},{11... | collective-permute-start | bytes 73736 | tf_op jit(solution)/shard_map/ppermute | solution.py:72
  30.9 3.1 %copy.255 = f32[24,64,4,1]{1,0,3,2:T(8,128)} copy(f32[24,64,4,1]{3,0,1,2:T(8,128)} %get-tuple-element.55) | data formatting | bytes 49152 | tf_op jit(solution)/shard_map/slice | solution.py:68
  34.0 2.2 collective-permute-start.16
  37.2 1.7 fusion.70
  39.5 4.3 %all-to-all-start = ((f32[4,1,16,128]{3,2,1,0:T(8,128)}), f32[4,1,16,128]{3,2,1,0:T(8,128)S(1)}, u32[]{:S(2)}, u32[]{:S(2)}) async-start(f32[4,1,16,128]{3,2,1,0:T(8,128)} %broadcast_in_dim.10), calls=%async_computation | async-start | bytes 65536 | tf_op jit(solution)/shard_map/all_to_all | solution.py:39
  43.9 1.9 slice_multiply_fusion
  50.0 2.7 %collective-permute-start.6 = (f32[3,16,16,1]{3,1,2,0:T(8,128)S(1)}, f32[3,16,16,1]{3,1,2,0:T(8,128)S(1)}, u32[]{:S(2)}, u32[]{:S(2)}) collective-permute-start(f32[3,16,16,1]{3,1,2,0:T(8,128)S(1)} %get-tuple-element.57), channel_id=1, source_target_pairs={{1,0},{2,1},{3,2},{4,3},{5,4},{6,5},{7,6},{9,8},{10,9},{11,10},{12... | collective-permute-start | bytes 9224 | tf_op jit(solution)/shard_map/ppermute | solution.py:26
  52.7 4.3 %collective-permute-start.4 = (f32[3,16,1,128]{3,1,2,0:T(8,128)S(1)}, f32[3,16,1,128]{3,1,2,0:T(8,128)S(1)}, u32[]{:S(2)}, u32[]{:S(2)}) collective-permute-start(f32[3,16,1,128]{3,1,2,0:T(8,128)S(1)} %get-tuple-element.61), channel_id=1, source_target_pairs={{8,0},{16,8},{24,16},{32,24},{40,32},{48,40},{56,48},{9,1},{17,9},... | collective-permute-start | bytes 73736 | tf_op jit(solution)/shard_map/ppermute | solution.py:26
  57.0 1.9 collective-permute-start.5
  59.1 6.0 %collective-permute-done.6 = f32[3,16,16,1]{3,1,2,0:T(8,128)S(1)} collective-permute-done((f32[3,16,16,1]{3,1,2,0:T(8,128)S(1)}, f32[3,16,16,1]{3,1,2,0:T(8,128)S(1)}, u32[]{:S(2)}, u32[]{:S(2)}) %collective-permute-start.6) | collective-permute-done | bytes 3104 | tf_op jit(solution)/shard_map/ppermute | solution.py:26
  67.8 1.8 fusion.48
  69.6 5.4 %all-to-all-start.2 = ((f32[16,16,128]{2,0,1:T(8,128)}), f32[16,16,128]{2,0,1:T(8,128)}, u32[]{:S(2)}, u32[]{:S(2)}) async-start(f32[16,16,128]{2,0,1:T(8,128)} %get-tuple-element.58), calls=%async_computation.2 | async-start | bytes 262144 | tf_op jit(solution)/shard_map/all_to_all | solution.py:139
  76.3 5.4 %copy.346 = f32[24,64,1,1,4,128]{5,0,4,1,2,3:T(8,128)} copy(f32[24,64,1,1,4,128]{5,4,3,2,1,0:T(4,128)} %param.19) | data formatting | bytes 6291456 | tf_op jit(solution)/shard_map/reshape | solution.py:166
  83.4 3.0 %copy.253 = f32[24,64,4,1]{3,0,1,2:T(8,128)} copy(f32[24,64,4,1]{1,0,3,2:T(8,128)} %collective-permute-done.15) | data formatting | bytes 49152 | tf_op jit(solution)/shard_map/ppermute | solution.py:72
  86.4 3.0 %copy.256 = f32[24,64,4,1]{3,0,1,2:T(8,128)} copy(f32[24,64,4,1]{1,0,3,2:T(8,128)} %collective-permute-done.16) | data formatting | bytes 49152 | tf_op jit(solution)/shard_map/ppermute | solution.py:74
  89.3 4.2 %all-to-all-start.1 = ((f32[16,16,128]{2,0,1:T(8,128)}), f32[16,16,128]{2,0,1:T(8,128)}, u32[]{:S(2)}, u32[]{:S(2)}) async-start(f32[16,16,128]{2,0,1:T(8,128)} %get-tuple-element.59), calls=%async_computation.1 | async-start | bytes 262144 | tf_op jit(solution)/shard_map/all_to_all | solution.py:138
  96.0 3.2 %collective-permute-start.14 = (f32[64,4]{0,1:T(4,128)}, f32[64,4]{0,1:T(4,128)}, u32[]{:S(2)}, u32[]{:S(2)}) collective-permute-start(f32[64,4]{0,1:T(4,128)} %slice_reduce_fusion), channel_id=1, source_target_pairs={{0,1},{1,2},{2,3},{3,4},{4,5},{5,6},{6,7},{8,9},{9,10},{10,11},{11... | collective-permute-start | bytes 3080 | tf_op jit(solution)/shard_map/ppermute | solution.py:56
  105.2 4.7 %pad_maximum_fusion = (f32[24,64,4,129]{3,0,1,2:T(8,128)S(1)}, f32[24,64,4,129]{3,0,1,2:T(8,128)S(1)}) fusion(f32[24,64,4,128]{3,0,1,2:T(8,128)S(1)} %bitcast.168, f32[24,64,4,1]{3,0,1,2:T(8,128)} %copy.253, f32[24,64,4,1]{3,0,1,2:T(8,128)} %copy.256, f32[64,4,129]{2,0,1:T(8,128)S(1)} %get-tuple-element.65), kind=kLoop, calls=%fused_computation | loop fusion | flops 2377728 | bytes 9667584 | tf_op jit(solution)/shard_map/concatenate | solution.py:70
  110.8 1.9 collective-permute-start.9
  112.7 4.3 %collective-permute-start.13 = (f32[24,64,128]{2,0,1:T(8,128)}, f32[24,64,128]{2,0,1:T(8,128)}, u32[]{:S(2)}, u32[]{:S(2)}) collective-permute-start(f32[24,64,128]{2,0,1:T(8,128)} %collective-permute-done.12), channel_id=1, source_target_pairs={{8,0},{16,8},{24,16},{32,24},{40,32},{48,40},{56,48},{9,1},{17,9},... | collective-permute-start | bytes 2359304 | tf_op jit(solution)/shard_map/ppermute | solution.py:56
  117.0 2.0 collective-permute-start.11
  118.9 4.6 %copy_add_fusion = f32[24,64,4,129]{3,0,2,1:T(8,128)} fusion(f32[24,64,4,129]{3,0,1,2:T(8,128)S(1)} %get-tuple-element.53, f32[24,64,4,129]{3,0,1,2:T(8,128)S(1)} %get-tuple-element.52, f32[64,4,129]{2,1,0:T(4,128)} %copy.251), kind=kLoop, calls=%fused_computation.5 | loop fusion | flops 1585152 | bytes 9643008 | tf_op jit(solution)/shard_map/add | solution.py:182
  126.1 25.4 %collective-permute-done.11 = f32[24,64,128]{2,0,1:T(8,128)} collective-permute-done((f32[24,64,128]{2,0,1:T(8,128)}, f32[24,64,128]{2,0,1:T(8,128)}, u32[]{:S(2)}, u32[]{:S(2)}) %collective-permute-start.11) | collective-permute-done | bytes 786464 | tf_op jit(solution)/shard_map/ppermute | solution.py:56
  155.8 6.8 %fusion.7 = f32[24,64,4,128]{3,0,2,1:T(8,128)S(1)} fusion(f32[24,64,4,129]{3,0,2,1:T(8,128)} %copy_add_fusion, f32[24,64,5,128]{3,0,2,1:T(8,128)S(1)} %fusion.1, f32[64,4,128]{2,1,0:T(4,128)} %copy.242, f32[24,64,1,1,4,128]{5,4,3,2,1,0:T(4,128)S(1)} %copy-done.1), kind=kLoop, calls=%fused_computation.20 | loop fusion | flops 3932160 | bytes 19005440 | tf_op jit(solution)/shard_map/mul | solution.py:186
  164.5 8.6 %collective-permute-start.7 = (f32[3,16,16,1]{3,1,2,0:T(8,128)S(1)}, f32[3,16,16,1]{3,1,2,0:T(8,128)S(1)}, u32[]{:S(2)}, u32[]{:S(2)}) collective-permute-start(f32[3,16,16,1]{3,1,2,0:T(8,128)S(1)} %copy-done.24), channel_id=1, source_target_pairs={{0,1},{1,2},{2,3},{3,4},{4,5},{5,6},{6,7},{8,9},{9,10},{10,11},{11... | collective-permute-start | bytes 9224 | tf_op jit(solution)/shard_map/ppermute | solution.py:25
  173.1 4.7 %collective-permute-done.7 = f32[3,16,16,1]{3,1,2,0:T(8,128)S(1)} collective-permute-done((f32[3,16,16,1]{3,1,2,0:T(8,128)S(1)}, f32[3,16,16,1]{3,1,2,0:T(8,128)S(1)}, u32[]{:S(2)}, u32[]{:S(2)}) %collective-permute-start.7) | collective-permute-done | bytes 3104 | tf_op jit(solution)/shard_map/ppermute | solution.py:25
  179.6 2.1 collective-permute-done.17
  181.7 3.4 %collective-permute-start.18 = (f32[24,64,128]{2,0,1:T(8,128)}, f32[24,64,128]{2,0,1:T(8,128)}, u32[]{:S(2)}, u32[]{:S(2)}) collective-permute-start(f32[24,64,128]{2,0,1:T(8,128)} %collective-permute-done.17), channel_id=1, source_target_pairs={{0,8},{8,16},{16,24},{24,32},{32,40},{40,48},{48,56},{1,9},{9,17},... | collective-permute-start | bytes 2359304 | tf_op jit(solution)/shard_map/ppermute | solution.py:56
  185.1 3.8 %fusion.71 = (f32[24,64,4,1]{3,0,2,1:T(8,128)}, f32[24,64,4,1]{3,0,2,1:T(8,128)}) fusion(f32[24,64,4,128]{3,0,2,1:T(8,128)S(1)} %fusion.7), kind=kLoop, calls=%fused_computation.156 | loop fusion | bytes 98304 | tf_op jit(solution)/shard_map/slice | solution.py:68
  188.9 3.3 %copy.263 = f32[24,64,4,1]{1,0,3,2:T(8,128)} copy(f32[24,64,4,1]{3,0,2,1:T(8,128)} %get-tuple-element.49) | data formatting | bytes 49152 | tf_op jit(solution)/shard_map/slice | solution.py:69
  192.2 8.4 %collective-permute-start.21 = (f32[24,64,4,1]{1,0,3,2:T(8,128)}, f32[24,64,4,1]{1,0,3,2:T(8,128)}, u32[]{:S(2)}, u32[]{:S(2)}) collective-permute-start(f32[24,64,4,1]{1,0,3,2:T(8,128)} %copy.263), channel_id=1, source_target_pairs={{0,1},{1,2},{2,3},{3,4},{4,5},{5,6},{6,7},{8,9},{9,10},{10,11},{11... | collective-permute-start | bytes 73736 | tf_op jit(solution)/shard_map/ppermute | solution.py:72
  200.5 3.2 %copy.265 = f32[24,64,4,1]{1,0,3,2:T(8,128)} copy(f32[24,64,4,1]{3,0,2,1:T(8,128)} %get-tuple-element.48) | data formatting | bytes 49152 | tf_op jit(solution)/shard_map/slice | solution.py:68
  203.8 1.9 collective-permute-start.22
  205.7 4.8 %collective-permute-start.20 = (f32[24,64,128]{2,0,1:T(8,128)}, f32[24,64,128]{2,0,1:T(8,128)}, u32[]{:S(2)}, u32[]{:S(2)}) collective-permute-start(f32[24,64,128]{2,0,1:T(8,128)} %collective-permute-done.19), channel_id=1, source_target_pairs={{8,0},{16,8},{24,16},{32,24},{40,32},{48,40},{56,48},{9,1},{17,9},... | collective-permute-start | bytes 2359304 | tf_op jit(solution)/shard_map/ppermute | solution.py:56
  215.3 3.2 %copy.264 = f32[24,64,4,1]{3,0,2,1:T(8,128)} copy(f32[24,64,4,1]{1,0,3,2:T(8,128)} %collective-permute-done.21) | data formatting | bytes 49152 | tf_op jit(solution)/shard_map/ppermute | solution.py:72
  218.5 3.2 %copy.266 = f32[24,64,4,1]{3,0,2,1:T(8,128)} copy(f32[24,64,4,1]{1,0,3,2:T(8,128)} %collective-permute-done.22) | data formatting | bytes 49152 | tf_op jit(solution)/shard_map/ppermute | solution.py:74
  221.6 4.3 %fusion = f32[24,64,4,129]{3,0,2,1:T(8,128)S(1)} fusion(f32[24,64,4,128]{3,0,2,1:T(8,128)S(1)} %fusion.7, f32[24,64,4,1]{3,0,2,1:T(8,128)} %copy.264, f32[24,64,4,1]{3,0,2,1:T(8,128)} %copy.266, f32[64,4,129]{2,1,0:T(4,128)} %copy.288, f32[64,4,129]{2,1,0:T(4,128)S(1)} %copy-done.8), kind=kLoop, calls=%fused_computation.3 | loop fusion | flops 3962880 | bytes 6629376 | tf_op jit(solution)/shard_map/add | solution.py:182
  232.7 1.7 fusion.67
  235.4 4.8 %all-to-all-start.3 = ((f32[64,4,128]{2,1,0:T(4,128)}), f32[64,4,128]{2,1,0:T(4,128)S(1)}, u32[]{:S(2)}, u32[]{:S(2)}) async-start(f32[64,4,128]{2,1,0:T(4,128)} %copy.271), calls=%async_computation.3 | async-start | bytes 262144 | tf_op jit(solution)/shard_map/all_to_all | solution.py:202
  240.4 7.0 %fusion.9 = f32[24,64,1,1,4,128]{5,0,4,1,3,2:T(8,128)S(1)} fusion(f32[24,64,4,128]{3,0,2,1:T(8,128)} %copy-done.2, f32[24]{0:T(128)} %param.24, f32[64,4,128]{2,1,0:T(4,128)S(1)} %copy.275, f32[24]{0:T(128)} %param.23, f32[64,4,128]{2,1,0:T(4,128)S(1)} %bitcast.184, f32[24]{0:T(128)} %param.22, f32[64,4,128]{2,1,0:T(4,128)S(1)} %copy.274, ...), kind=kOutput, calls=%fused_computation.24 | convolution fusion | flops 233570304 | bytes 6687264 | tf_op jit(solution)/shard_map/dot_general | solution.py:210
  247.4 2.5 copy.281
  (157 shorter events, 50.2 us)
Async XLA Ops:
  0.6 239.7 %copy-start = (f32[24,24]{1,0:T(8,128)S(1)}, f32[24,24]{1,0:T(8,128)}, u32[]{:S(2)}) copy-start(f32[24,24]{1,0:T(8,128)} %param.25) | copy-start | bytes 6916
  1.5 32.5 %collective-permute-start.3 = (s32[2,16,1]{2,1,0:T(8,128)S(1)}, s32[2,16,1]{2,1,0:T(8,128)S(1)}, u32[]{:S(2)}, u32[]{:S(2)}) collective-permute-start(s32[2,16,1]{2,1,0:T(8,128)S(1)} %get-tuple-element.73), channel_id=1, source_target_pairs={{1,0},{2,1},{3,2},{4,3},{5,4},{6,5},{7,6},{9,8},{10,9},{11,10},{12... | collective-permute-start | bytes 392 | tf_op jit(solution)/shard_map/ppermute | solution.py:26
  4.1 32.1 %collective-permute-start = (s32[2,16,1]{2,1,0:T(8,128)S(1)}, s32[2,16,1]{2,1,0:T(8,128)S(1)}, u32[]{:S(2)}, u32[]{:S(2)}) collective-permute-start(s32[2,16,1]{2,1,0:T(8,128)S(1)} %get-tuple-element.72), channel_id=1, source_target_pairs={{0,1},{1,2},{2,3},{3,4},{4,5},{5,6},{6,7},{8,9},{9,10},{10,11},{11... | collective-permute-start | bytes 392 | tf_op jit(solution)/shard_map/ppermute | solution.py:25
  9.6 26.6 %collective-permute-start.2 = (s32[2,1,128]{2,1,0:T(1,128)S(1)}, s32[2,1,128]{2,1,0:T(1,128)S(1)}, u32[]{:S(2)}, u32[]{:S(2)}) collective-permute-start(s32[2,1,128]{2,1,0:T(1,128)S(1)} %get-tuple-element.71), channel_id=1, source_target_pairs={{8,0},{16,8},{24,16},{32,24},{40,32},{48,40},{56,48},{9,1},{17,9},... | collective-permute-start | bytes 3080 | tf_op jit(solution)/shard_map/ppermute | solution.py:26
  13.4 22.8 %collective-permute-start.1 = (s32[2,1,128]{2,1,0:T(1,128)S(1)}, s32[2,1,128]{2,1,0:T(1,128)S(1)}, u32[]{:S(2)}, u32[]{:S(2)}) collective-permute-start(s32[2,1,128]{2,1,0:T(1,128)S(1)} %get-tuple-element.70), channel_id=1, source_target_pairs={{0,8},{8,16},{16,24},{24,32},{32,40},{40,48},{48,56},{1,9},{9,17},... | collective-permute-start | bytes 3080 | tf_op jit(solution)/shard_map/ppermute | solution.py:25
  22.7 7.6 %copy-start.31 = (s32[16,128]{1,0:T(8,128)S(1)}, s32[16,128]{1,0:T(8,128)}, u32[]{:S(2)}) copy-start(s32[16,128]{1,0:T(8,128)} %param.18) | copy-start | bytes 24580
  22.7 7.6 %copy-start.30 = (s32[16,128]{1,0:T(8,128)S(1)}, s32[16,128]{1,0:T(8,128)}, u32[]{:S(2)}) copy-start(s32[16,128]{1,0:T(8,128)} %param.17) | copy-start | bytes 24580
  25.8 57.5 %collective-permute-start.15 = (f32[24,64,4,1]{1,0,3,2:T(8,128)}, f32[24,64,4,1]{1,0,3,2:T(8,128)}, u32[]{:S(2)}, u32[]{:S(2)}) collective-permute-start(f32[24,64,4,1]{1,0,3,2:T(8,128)} %copy.252), channel_id=1, source_target_pairs={{0,1},{1,2},{2,3},{3,4},{4,5},{5,6},{6,7},{8,9},{9,10},{10,11},{11... | collective-permute-start | bytes 73736 | tf_op jit(solution)/shard_map/ppermute | solution.py:72
  28.5 8.7 %copy-start.29 = (f32[16,16,128]{2,1,0:T(8,128)S(1)}, f32[16,16,128]{2,1,0:T(8,128)}, u32[]{:S(2)}) copy-start(f32[16,16,128]{2,1,0:T(8,128)} %param.16) | copy-start | bytes 393220
  34.0 52.4 %collective-permute-start.16 = (f32[24,64,4,1]{1,0,3,2:T(8,128)}, f32[24,64,4,1]{1,0,3,2:T(8,128)}, u32[]{:S(2)}, u32[]{:S(2)}) collective-permute-start(f32[24,64,4,1]{1,0,3,2:T(8,128)} %copy.255), channel_id=1, source_target_pairs={{1,0},{2,1},{3,2},{4,3},{5,4},{6,5},{7,6},{9,8},{10,9},{11,10},{12... | collective-permute-start | bytes 73736 | tf_op jit(solution)/shard_map/ppermute | solution.py:74
  39.5 7.5 %all-to-all-start = ((f32[4,1,16,128]{3,2,1,0:T(8,128)}), f32[4,1,16,128]{3,2,1,0:T(8,128)S(1)}, u32[]{:S(2)}, u32[]{:S(2)}) async-start(f32[4,1,16,128]{3,2,1,0:T(8,128)} %broadcast_in_dim.10), calls=%async_computation | async-start | bytes 65536 | tf_op jit(solution)/shard_map/all_to_all | solution.py:39
  47.0 11.9 %copy-start.5 = (f32[16,18,130]{2,0,1:T(8,128)S(1)}, f32[16,18,130]{2,0,1:T(8,128)}, u32[]{:S(2)}) copy-start(f32[16,18,130]{2,0,1:T(8,128)} %copy-done.4) | copy-start | bytes 449284
  47.1 20.7 %copy-start.12 = (f32[16,16,129]{2,0,1:T(8,128)S(1)}, f32[16,16,129]{2,0,1:T(8,128)}, u32[]{:S(2)}) copy-start(f32[16,16,129]{2,0,1:T(8,128)} %slice_multiply_fusion) | copy-start | bytes 396292
  50.0 15.1 %collective-permute-start.6 = (f32[3,16,16,1]{3,1,2,0:T(8,128)S(1)}, f32[3,16,16,1]{3,1,2,0:T(8,128)S(1)}, u32[]{:S(2)}, u32[]{:S(2)}) collective-permute-start(f32[3,16,16,1]{3,1,2,0:T(8,128)S(1)} %get-tuple-element.57), channel_id=1, source_target_pairs={{1,0},{2,1},{3,2},{4,3},{5,4},{6,5},{7,6},{9,8},{10,9},{11,10},{12... | collective-permute-start | bytes 9224 | tf_op jit(solution)/shard_map/ppermute | solution.py:26
  52.7 14.0 %collective-permute-start.4 = (f32[3,16,1,128]{3,1,2,0:T(8,128)S(1)}, f32[3,16,1,128]{3,1,2,0:T(8,128)S(1)}, u32[]{:S(2)}, u32[]{:S(2)}) collective-permute-start(f32[3,16,1,128]{3,1,2,0:T(8,128)S(1)} %get-tuple-element.61), channel_id=1, source_target_pairs={{8,0},{16,8},{24,16},{32,24},{40,32},{48,40},{56,48},{9,1},{17,9},... | collective-permute-start | bytes 73736 | tf_op jit(solution)/shard_map/ppermute | solution.py:26
  57.0 9.7 %collective-permute-start.5 = (f32[3,16,1,128]{3,1,2,0:T(8,128)S(1)}, f32[3,16,1,128]{3,1,2,0:T(8,128)S(1)}, u32[]{:S(2)}, u32[]{:S(2)}) collective-permute-start(f32[3,16,1,128]{3,1,2,0:T(8,128)S(1)} %get-tuple-element.60), channel_id=1, source_target_pairs={{0,8},{8,16},{16,24},{24,32},{32,40},{40,48},{48,56},{1,9},{9,17},... | collective-permute-start | bytes 73736 | tf_op jit(solution)/shard_map/ppermute | solution.py:25
  59.1 10.5 %copy-start.18 = (f32[16,17,128]{2,0,1:T(8,128)}, f32[16,17,128]{2,0,1:T(8,128)S(1)}, u32[]{:S(2)}) copy-start(f32[16,17,128]{2,0,1:T(8,128)S(1)} %slice_multiply_fusion.1) | copy-start | bytes 417796
  65.1 47.6 %collective-permute-start.12 = (f32[24,64,128]{2,0,1:T(8,128)}, f32[24,64,128]{2,0,1:T(8,128)}, u32[]{:S(2)}, u32[]{:S(2)}) collective-permute-start(f32[24,64,128]{2,0,1:T(8,128)} %get-tuple-element.51), channel_id=1, source_target_pairs={{0,192},{64,0},{128,64},{192,128},{1,193},{65,1},{129,65},{193,129... | collective-permute-start | bytes 2359304 | tf_op jit(solution)/shard_map/ppermute | solution.py:61
  66.7 50.2 %collective-permute-start.10 = (f32[24,64,128]{2,0,1:T(8,128)}, f32[24,64,128]{2,0,1:T(8,128)}, u32[]{:S(2)}, u32[]{:S(2)}) collective-permute-start(f32[24,64,128]{2,0,1:T(8,128)} %get-tuple-element.50), channel_id=1, source_target_pairs={{0,64},{64,128},{128,192},{192,0},{1,65},{65,129},{129,193},{193,1... | collective-permute-start | bytes 2359304 | tf_op jit(solution)/shard_map/ppermute | solution.py:61
  69.6 19.7 %all-to-all-start.2 = ((f32[16,16,128]{2,0,1:T(8,128)}), f32[16,16,128]{2,0,1:T(8,128)}, u32[]{:S(2)}, u32[]{:S(2)}) async-start(f32[16,16,128]{2,0,1:T(8,128)} %get-tuple-element.58), calls=%async_computation.2 | async-start | bytes 262144 | tf_op jit(solution)/shard_map/all_to_all | solution.py:139
  89.3 9.9 %all-to-all-start.1 = ((f32[16,16,128]{2,0,1:T(8,128)}), f32[16,16,128]{2,0,1:T(8,128)}, u32[]{:S(2)}, u32[]{:S(2)}) async-start(f32[16,16,128]{2,0,1:T(8,128)} %get-tuple-element.59), calls=%async_computation.1 | async-start | bytes 262144 | tf_op jit(solution)/shard_map/all_to_all | solution.py:138
  96.0 6.6 %collective-permute-start.14 = (f32[64,4]{0,1:T(4,128)}, f32[64,4]{0,1:T(4,128)}, u32[]{:S(2)}, u32[]{:S(2)}) collective-permute-start(f32[64,4]{0,1:T(4,128)} %slice_reduce_fusion), channel_id=1, source_target_pairs={{0,1},{1,2},{2,3},{3,4},{4,5},{5,6},{6,7},{8,9},{9,10},{10,11},{11... | collective-permute-start | bytes 3080 | tf_op jit(solution)/shard_map/ppermute | solution.py:56
  101.4 9.3 %collective-permute-start.8 = (f32[64,128]{1,0:T(8,128)}, f32[64,128]{1,0:T(8,128)}, u32[]{:S(2)}, u32[]{:S(2)}) collective-permute-start(f32[64,128]{1,0:T(8,128)} %slice_bitcast_fusion.7), channel_id=1, source_target_pairs={{0,64},{64,128},{128,192},{192,0},{1,65},{65,129},{129,193},{193,1... | collective-permute-start | bytes 98312 | tf_op jit(solution)/shard_map/ppermute | solution.py:61
  105.2 4.7 %copy-start.9 = (f32[64,4,129]{2,0,1:T(8,128)}, f32[64,4,129]{2,0,1:T(8,128)S(1)}, u32[]{:S(2)}) copy-start(f32[64,4,129]{2,0,1:T(8,128)S(1)} %get-tuple-element.65) | copy-start | bytes 396292
  110.8 12.8 %collective-permute-start.9 = (f32[64,128]{1,0:T(8,128)}, f32[64,128]{1,0:T(8,128)S(1)}, u32[]{:S(2)}, u32[]{:S(2)}) collective-permute-start(f32[64,128]{1,0:T(8,128)} %collective-permute-done.8), channel_id=1, source_target_pairs={{0,8},{8,16},{16,24},{24,32},{32,40},{40,48},{48,56},{1,9},{9,17},... | collective-permute-start | bytes 98312 | tf_op jit(solution)/shard_map/ppermute | solution.py:56
  112.7 40.0 %collective-permute-start.13 = (f32[24,64,128]{2,0,1:T(8,128)}, f32[24,64,128]{2,0,1:T(8,128)}, u32[]{:S(2)}, u32[]{:S(2)}) collective-permute-start(f32[24,64,128]{2,0,1:T(8,128)} %collective-permute-done.12), channel_id=1, source_target_pairs={{8,0},{16,8},{24,16},{32,24},{40,32},{48,40},{56,48},{9,1},{17,9},... | collective-permute-start | bytes 2359304 | tf_op jit(solution)/shard_map/ppermute | solution.py:56
  117.0 34.5 %collective-permute-start.11 = (f32[24,64,128]{2,0,1:T(8,128)}, f32[24,64,128]{2,0,1:T(8,128)}, u32[]{:S(2)}, u32[]{:S(2)}) collective-permute-start(f32[24,64,128]{2,0,1:T(8,128)} %collective-permute-done.10), channel_id=1, source_target_pairs={{0,8},{8,16},{16,24},{24,32},{32,40},{40,48},{48,56},{1,9},{9,17},... | collective-permute-start | bytes 2359304 | tf_op jit(solution)/shard_map/ppermute | solution.py:56
  123.5 30.4 %copy-start.3 = (f32[24,64,1,1,4,128]{5,0,4,1,2,3:T(8,128)S(1)}, f32[24,64,1,1,4,128]{5,0,4,1,2,3:T(8,128)}, u32[]{:S(2)}) copy-start(f32[24,64,1,1,4,128]{5,0,4,1,2,3:T(8,128)} %copy.346) | copy-start | bytes 9437188
  125.4 28.5 %copy-start.16 = (f32[64,5,128]{2,0,1:T(8,128)}, f32[64,5,128]{2,0,1:T(8,128)S(1)}, u32[]{:S(2)}) copy-start(f32[64,5,128]{2,0,1:T(8,128)S(1)} %get-tuple-element.67) | copy-start | bytes 491524
  162.6 15.3 %copy-start.7 = (f32[3,16,18,129]{3,1,2,0:T(8,128)S(1)}, f32[3,16,18,129]{3,1,2,0:T(8,128)}, u32[]{:S(2)}) copy-start(f32[3,16,18,129]{3,1,2,0:T(8,128)} %copy-done.6) | copy-start | bytes 1337476
  162.6 15.3 %copy-start.13 = (f32[16,16,129]{2,0,1:T(8,128)S(1)}, f32[16,16,129]{2,0,1:T(8,128)}, u32[]{:S(2)}) copy-start(f32[16,16,129]{2,0,1:T(8,128)} %slice_multiply_fusion) | copy-start | bytes 396292
  162.6 15.3 %copy-start.26 = (f32[3,16,1,128]{3,1,2,0:T(8,128)S(1)}, f32[3,16,1,128]{3,1,2,0:T(8,128)}, u32[]{:S(2)}) copy-start(f32[3,16,1,128]{3,1,2,0:T(8,128)} %copy-done.25) | copy-start | bytes 73732
  162.6 15.2 %copy-start.28 = (f32[3,16,1,128]{3,1,2,0:T(8,128)S(1)}, f32[3,16,1,128]{3,1,2,0:T(8,128)}, u32[]{:S(2)}) copy-start(f32[3,16,1,128]{3,1,2,0:T(8,128)} %copy-done.27) | copy-start | bytes 73732
  162.6 16.1 %copy-start.19 = (f32[16,17,128]{2,0,1:T(8,128)S(1)}, f32[16,17,128]{2,0,1:T(8,128)}, u32[]{:S(2)}) copy-start(f32[16,17,128]{2,0,1:T(8,128)} %copy-done.18) | copy-start | bytes 417796
  163.6 18.1 %collective-permute-start.17 = (f32[24,64,128]{2,0,1:T(8,128)S(1)}, f32[24,64,128]{2,0,1:T(8,128)}, u32[]{:S(2)}, u32[]{:S(2)}) collective-permute-start(f32[24,64,128]{2,0,1:T(8,128)S(1)} %get-tuple-element.47), channel_id=1, source_target_pairs={{0,64},{64,128},{128,192},{192,0},{1,65},{65,129},{129,193},{193,1... | collective-permute-start | bytes 2359304 | tf_op jit(solution)/shard_map/ppermute | solution.py:61
  164.5 13.3 %collective-permute-start.7 = (f32[3,16,16,1]{3,1,2,0:T(8,128)S(1)}, f32[3,16,16,1]{3,1,2,0:T(8,128)S(1)}, u32[]{:S(2)}, u32[]{:S(2)}) collective-permute-start(f32[3,16,16,1]{3,1,2,0:T(8,128)S(1)} %copy-done.24), channel_id=1, source_target_pairs={{0,1},{1,2},{2,3},{3,4},{4,5},{5,6},{6,7},{8,9},{9,10},{10,11},{11... | collective-permute-start | bytes 9224 | tf_op jit(solution)/shard_map/ppermute | solution.py:25
  178.1 27.6 %collective-permute-start.19 = (f32[24,64,128]{2,0,1:T(8,128)}, f32[24,64,128]{2,0,1:T(8,128)}, u32[]{:S(2)}, u32[]{:S(2)}) collective-permute-start(f32[24,64,128]{2,0,1:T(8,128)} %get-tuple-element.46), channel_id=1, source_target_pairs={{0,192},{64,0},{128,64},{192,128},{1,193},{65,1},{129,65},{193,129... | collective-permute-start | bytes 2359304 | tf_op jit(solution)/shard_map/ppermute | solution.py:61
  181.7 44.3 %collective-permute-start.18 = (f32[24,64,128]{2,0,1:T(8,128)}, f32[24,64,128]{2,0,1:T(8,128)}, u32[]{:S(2)}, u32[]{:S(2)}) collective-permute-start(f32[24,64,128]{2,0,1:T(8,128)} %collective-permute-done.17), channel_id=1, source_target_pairs={{0,8},{8,16},{16,24},{24,32},{32,40},{40,48},{48,56},{1,9},{9,17},... | collective-permute-start | bytes 2359304 | tf_op jit(solution)/shard_map/ppermute | solution.py:56
  188.9 24.1 %copy-start.21 = (f32[16,16,128]{2,0,1:T(8,128)S(1)}, f32[16,16,128]{2,0,1:T(8,128)}, u32[]{:S(2)}) copy-start(f32[16,16,128]{2,0,1:T(8,128)} %get-tuple-element.58) | copy-start | bytes 393220
  188.9 25.5 %copy-start.10 = (f32[64,4,129]{2,0,1:T(8,128)S(1)}, f32[64,4,129]{2,0,1:T(8,128)}, u32[]{:S(2)}) copy-start(f32[64,4,129]{2,0,1:T(8,128)} %copy-done.9) | copy-start | bytes 396292
  192.2 23.1 %collective-permute-start.21 = (f32[24,64,4,1]{1,0,3,2:T(8,128)}, f32[24,64,4,1]{1,0,3,2:T(8,128)}, u32[]{:S(2)}, u32[]{:S(2)}) collective-permute-start(f32[24,64,4,1]{1,0,3,2:T(8,128)} %copy.263), channel_id=1, source_target_pairs={{0,1},{1,2},{2,3},{3,4},{4,5},{5,6},{6,7},{8,9},{9,10},{10,11},{11... | collective-permute-start | bytes 73736 | tf_op jit(solution)/shard_map/ppermute | solution.py:72
  203.8 14.7 %collective-permute-start.22 = (f32[24,64,4,1]{1,0,3,2:T(8,128)}, f32[24,64,4,1]{1,0,3,2:T(8,128)}, u32[]{:S(2)}, u32[]{:S(2)}) collective-permute-start(f32[24,64,4,1]{1,0,3,2:T(8,128)} %copy.265), channel_id=1, source_target_pairs={{1,0},{2,1},{3,2},{4,3},{5,4},{6,5},{7,6},{9,8},{10,9},{11,10},{12... | collective-permute-start | bytes 73736 | tf_op jit(solution)/shard_map/ppermute | solution.py:74
  205.7 21.6 %collective-permute-start.20 = (f32[24,64,128]{2,0,1:T(8,128)}, f32[24,64,128]{2,0,1:T(8,128)}, u32[]{:S(2)}, u32[]{:S(2)}) collective-permute-start(f32[24,64,128]{2,0,1:T(8,128)} %collective-permute-done.19), channel_id=1, source_target_pairs={{8,0},{16,8},{24,16},{32,24},{40,32},{48,40},{56,48},{9,1},{17,9},... | collective-permute-start | bytes 2359304 | tf_op jit(solution)/shard_map/ppermute | solution.py:56
  215.3 6.4 %copy-start.8 = (f32[64,4,129]{2,1,0:T(4,128)S(1)}, f32[64,4,129]{2,1,0:T(4,128)}, u32[]{:S(2)}) copy-start(f32[64,4,129]{2,1,0:T(4,128)} %copy.251) | copy-start | bytes 396292
  229.6 3.1 %copy-start.33 = (f32[24]{0:T(128)S(1)}, f32[24]{0:T(128)}, u32[]{:S(2)}) copy-start(f32[24]{0:T(128)} %param.21) | copy-start | bytes 292
  231.0 3.4 %copy-start.32 = (pred[4,128]{1,0:T(4,128)(4,1)S(1)}, pred[4,128]{1,0:T(4,128)(4,1)}, u32[]{:S(2)}) copy-start(pred[4,128]{1,0:T(4,128)(4,1)} %dynamic-slice_compare_fusion) | copy-start | bytes 1540
  231.0 3.4 %copy-start.34 = (f32[1,1,4,128]{3,2,1,0:T(4,128)S(1)}, f32[1,1,4,128]{3,2,1,0:T(4,128)}, u32[]{:S(2)}) copy-start(f32[1,1,4,128]{3,2,1,0:T(4,128)} %param.20) | copy-start | bytes 6148
  235.4 14.5 %all-to-all-start.3 = ((f32[64,4,128]{2,1,0:T(4,128)}), f32[64,4,128]{2,1,0:T(4,128)S(1)}, u32[]{:S(2)}, u32[]{:S(2)}) async-start(f32[64,4,128]{2,1,0:T(4,128)} %copy.271), calls=%async_computation.3 | async-start | bytes 262144 | tf_op jit(solution)/shard_map/all_to_all | solution.py:202
  (14 other events, 23.6 us)
where the time goes:
time: 254 us; the launch traced here: 252 us
  starting transfers between devices  88.2 us (35%)
  local copies, waits for them, and re-layouts  66.7 us (26%)
  other arithmetic  46.3 us (18%)
  waiting for transfers between devices  39.6 us (16%)
  matrix products  10.1 us (4%)
    ppermute x6, waiting for transfers between devices, from_behind(): return lax.ppermute(x, axis, pairs)  25.4 us
    ppermute x6, starting transfers between devices, from_behind(): return lax.ppermute(x, axis, pairs)  19.5 us
    unnamed x79, local copies, waits for them, and re-layouts  17.6 us
    ppermute x4, starting transfers between devices, padded(): lax.ppermute(last, axis, up)  17.2 us
    ppermute x4, starting transfers between devices, padded(): lax.ppermute(first, axis, [(b, a) for a, b in up])  13.3 us
    ppermute x2, starting transfers between devices, extended_2(): lax.ppermute(tail, axis, [(i, (i + 1) % count) for i in range(ends)])  11 us
    slice x3, local copies, waits for them, and re-layouts, extended_2(): head = lax.slice_in_dim(cells, 0, width, axis=dim)  10.1 us
    slice x3, local copies, waits for them, and re-layouts, extended_2(): lax.slice_in_dim(cells, cells.shape[dim] - width, cells.shape[dim], axis=...  10 us
  transfers between devices with their start and end apart: 27, of which 5 were waited for; matrix products, arithmetic and copies ran while one was open for 39% of the time, Pallas kernels for 0%

commit v1 on v0

--- a/solution.py
+++ b/solution.py
@@ -136,7 +136,12 @@
     )
     east_column, north_column = (
         lax.all_to_all(east_new, "comp", split_axis=1, concat_axis=0, tiled=True),
-        lax.all_to_all(north_new, "comp", split_axis=1, concat_axis=0, tiled=True),
+        jnp.concatenate(
+            lax.all_to_all(
+                jnp.stack(jnp.split(north_new, lax.psum(1, "comp"), axis=1)), "comp", 0, 0
+            ),
+            axis=0,
+        ),
     )
     scalar_pair = padded_field[:2]
     flux_east = face_east[None] * (scalar_pair[:, :, 1:, 1:-1] - scalar_pair[:, :, :-1, 1:-1])

time: 254 us -> 256 us (level)
    unnamed x79 -> x81, local copies, waits for them, and re-layouts: 17.6 us -> 18.3 us
where the time goes in v1:
time: 256 us; the launch traced here: 254 us
  starting transfers between devices  88.1 us (34%)
  local copies, waits for them, and re-layouts  67.4 us (26%)
  other arithmetic  46.9 us (18%)
  waiting for transfers between devices  39.7 us (16%)
  matrix products  10.1 us (4%)
    ppermute x6, waiting for transfers between devices, from_behind(): return lax.ppermute(x, axis, pairs)  25.5 us
    ppermute x6, starting transfers between devices, from_behind(): return lax.ppermute(x, axis, pairs)  19.5 us
    unnamed x81, local copies, waits for them, and re-layouts  18.3 us
    ppermute x4, starting transfers between devices, padded(): lax.ppermute(last, axis, up)  17.2 us
    ppermute x4, starting transfers between devices, padded(): lax.ppermute(first, axis, [(b, a) for a, b in up])  13.3 us
    ppermute x2, starting transfers between devices, extended_2(): lax.ppermute(tail, axis, [(i, (i + 1) % count) for i in range(ends)])  11 us
    slice x3, local copies, waits for them, and re-layouts, extended_2(): head = lax.slice_in_dim(cells, 0, width, axis=dim)  10.1 us
    slice x3, local copies, waits for them, and re-layouts, extended_2(): lax.slice_in_dim(cells, cells.shape[dim] - width, cells.shape[dim], axis=...  10.1 us
  transfers between devices with their start and end apart: 27, of which 5 were waited for; matrix products, arithmetic and copies ran while one was open for 39% of the time, Pallas kernels for 0%

profile of v1, /device:TPU:15, one launch (start us, length us, event | category | flops | bytes accessed | tf_op | source)
XLA Modules:
  0.0 253.7 jit_solution(1476905875196535893)
XLA Ops:
  1.5 2.6 %collective-permute-start.3 = (s32[2,16,1]{2,1,0:T(8,128)S(1)}, s32[2,16,1]{2,1,0:T(8,128)S(1)}, u32[]{:S(2)}, u32[]{:S(2)}) collective-permute-start(s32[2,16,1]{2,1,0:T(8,128)S(1)} %get-tuple-element.77), channel_id=1, source_target_pairs={{1,0},{2,1},{3,2},{4,3},{5,4},{6,5},{7,6},{9,8},{10,9},{11,10},{12... | collective-permute-start | bytes 392 | tf_op jit(solution)/shard_map/ppermute | solution.py:26
  4.1 4.8 %collective-permute-start = (s32[2,16,1]{2,1,0:T(8,128)S(1)}, s32[2,16,1]{2,1,0:T(8,128)S(1)}, u32[]{:S(2)}, u32[]{:S(2)}) collective-permute-start(s32[2,16,1]{2,1,0:T(8,128)S(1)} %get-tuple-element.76), channel_id=1, source_target_pairs={{0,1},{1,2},{2,3},{3,4},{4,5},{5,6},{6,7},{8,9},{9,10},{10,11},{11... | collective-permute-start | bytes 392 | tf_op jit(solution)/shard_map/ppermute | solution.py:25
  9.6 3.8 %collective-permute-start.2 = (s32[2,1,128]{2,1,0:T(1,128)S(1)}, s32[2,1,128]{2,1,0:T(1,128)S(1)}, u32[]{:S(2)}, u32[]{:S(2)}) collective-permute-start(s32[2,1,128]{2,1,0:T(1,128)S(1)} %get-tuple-element.75), channel_id=1, source_target_pairs={{8,0},{16,8},{24,16},{32,24},{40,32},{48,40},{56,48},{9,1},{17,9},... | collective-permute-start | bytes 3080 | tf_op jit(solution)/shard_map/ppermute | solution.py:26
  13.4 1.9 collective-permute-start.1
  15.4 3.7 %copy.347 = f32[24,64,1,1,4,128]{5,0,1,4,3,2:T(8,128)S(1)} copy(f32[24,64,1,1,4,128]{5,4,3,2,1,0:T(4,128)} %param.19) | data formatting | bytes 6291456 | tf_op args[6]
  19.1 3.7 %fusion.72 = (f32[24,64,4,1]{3,0,1,2:T(8,128)}, f32[24,64,4,1]{3,0,1,2:T(8,128)}) fusion(f32[24,64,4,128]{3,0,1,2:T(8,128)S(1)} %bitcast.171), kind=kLoop, calls=%fused_computation.162 | loop fusion | bytes 98304 | tf_op jit(solution)/shard_map/slice | solution.py:69
  22.7 3.1 %copy.252 = f32[24,64,4,1]{1,0,3,2:T(8,128)} copy(f32[24,64,4,1]{3,0,1,2:T(8,128)} %get-tuple-element.54) | data formatting | bytes 49152 | tf_op jit(solution)/shard_map/slice | solution.py:69
  25.9 2.7 %collective-permute-start.15 = (f32[24,64,4,1]{1,0,3,2:T(8,128)}, f32[24,64,4,1]{1,0,3,2:T(8,128)}, u32[]{:S(2)}, u32[]{:S(2)}) collective-permute-start(f32[24,64,4,1]{1,0,3,2:T(8,128)} %copy.252), channel_id=1, source_target_pairs={{0,1},{1,2},{2,3},{3,4},{4,5},{5,6},{6,7},{8,9},{9,10},{10,11},{11... | collective-permute-start | bytes 73736 | tf_op jit(solution)/shard_map/ppermute | solution.py:72
  30.9 3.1 %copy.255 = f32[24,64,4,1]{1,0,3,2:T(8,128)} copy(f32[24,64,4,1]{3,0,1,2:T(8,128)} %get-tuple-element.55) | data formatting | bytes 49152 | tf_op jit(solution)/shard_map/slice | solution.py:68
  34.0 2.2 collective-permute-start.16
  37.2 1.7 fusion.70
  39.5 4.3 %all-to-all-start = ((f32[4,1,16,128]{3,2,1,0:T(8,128)}), f32[4,1,16,128]{3,2,1,0:T(8,128)S(1)}, u32[]{:S(2)}, u32[]{:S(2)}) async-start(f32[4,1,16,128]{3,2,1,0:T(8,128)} %broadcast_in_dim.10), calls=%async_computation | async-start | bytes 65536 | tf_op jit(solution)/shard_map/all_to_all | solution.py:39
  43.9 1.9 slice_multiply_fusion
  50.0 2.7 %collective-permute-start.6 = (f32[3,16,16,1]{3,1,2,0:T(8,128)S(1)}, f32[3,16,16,1]{3,1,2,0:T(8,128)S(1)}, u32[]{:S(2)}, u32[]{:S(2)}) collective-permute-start(f32[3,16,16,1]{3,1,2,0:T(8,128)S(1)} %get-tuple-element.57), channel_id=1, source_target_pairs={{1,0},{2,1},{3,2},{4,3},{5,4},{6,5},{7,6},{9,8},{10,9},{11,10},{12... | collective-permute-start | bytes 9224 | tf_op jit(solution)/shard_map/ppermute | solution.py:26
  52.7 4.3 %collective-permute-start.4 = (f32[3,16,1,128]{3,1,2,0:T(8,128)S(1)}, f32[3,16,1,128]{3,1,2,0:T(8,128)S(1)}, u32[]{:S(2)}, u32[]{:S(2)}) collective-permute-start(f32[3,16,1,128]{3,1,2,0:T(8,128)S(1)} %get-tuple-element.61), channel_id=1, source_target_pairs={{8,0},{16,8},{24,16},{32,24},{40,32},{48,40},{56,48},{9,1},{17,9},... | collective-permute-start | bytes 73736 | tf_op jit(solution)/shard_map/ppermute | solution.py:26
  57.0 1.9 collective-permute-start.5
  59.1 6.0 %collective-permute-done.6 = f32[3,16,16,1]{3,1,2,0:T(8,128)S(1)} collective-permute-done((f32[3,16,16,1]{3,1,2,0:T(8,128)S(1)}, f32[3,16,16,1]{3,1,2,0:T(8,128)S(1)}, u32[]{:S(2)}, u32[]{:S(2)}) %collective-permute-start.6) | collective-permute-done | bytes 3104 | tf_op jit(solution)/shard_map/ppermute | solution.py:26
  67.8 1.8 fusion.48
  70.9 5.4 %all-to-all-start.2 = ((f32[4,16,4,128]{3,1,2,0:T(8,128)}), f32[4,16,4,128]{3,1,2,0:T(8,128)}, u32[]{:S(2)}, u32[]{:S(2)}) async-start(f32[4,16,4,128]{3,1,2,0:T(8,128)} %pad_maximum_fusion.14), calls=%async_computation.2 | async-start | bytes 262144 | tf_op jit(solution)/shard_map/all_to_all | solution.py:140
  77.6 5.4 %copy.346 = f32[24,64,1,1,4,128]{5,0,4,1,2,3:T(8,128)} copy(f32[24,64,1,1,4,128]{5,4,3,2,1,0:T(4,128)} %param.19) | data formatting | bytes 6291456 | tf_op jit(solution)/shard_map/reshape | solution.py:171
  84.6 3.0 %copy.253 = f32[24,64,4,1]{3,0,1,2:T(8,128)} copy(f32[24,64,4,1]{1,0,3,2:T(8,128)} %collective-permute-done.15) | data formatting | bytes 49152 | tf_op jit(solution)/shard_map/ppermute | solution.py:72
  87.6 3.0 %copy.256 = f32[24,64,4,1]{3,0,1,2:T(8,128)} copy(f32[24,64,4,1]{1,0,3,2:T(8,128)} %collective-permute-done.16) | data formatting | bytes 49152 | tf_op jit(solution)/shard_map/ppermute | solution.py:74
  90.6 4.2 %all-to-all-start.1 = ((f32[16,16,128]{2,0,1:T(8,128)}), f32[16,16,128]{2,0,1:T(8,128)}, u32[]{:S(2)}, u32[]{:S(2)}) async-start(f32[16,16,128]{2,0,1:T(8,128)} %get-tuple-element.59), calls=%async_computation.1 | async-start | bytes 262144 | tf_op jit(solution)/shard_map/all_to_all | solution.py:138
  97.2 3.2 %collective-permute-start.14 = (f32[64,4]{0,1:T(4,128)}, f32[64,4]{0,1:T(4,128)}, u32[]{:S(2)}, u32[]{:S(2)}) collective-permute-start(f32[64,4]{0,1:T(4,128)} %slice_reduce_fusion), channel_id=1, source_target_pairs={{0,1},{1,2},{2,3},{3,4},{4,5},{5,6},{6,7},{8,9},{9,10},{10,11},{11... | collective-permute-start | bytes 3080 | tf_op jit(solution)/shard_map/ppermute | solution.py:56
  106.4 4.7 %pad_maximum_fusion = (f32[24,64,4,129]{3,0,1,2:T(8,128)S(1)}, f32[24,64,4,129]{3,0,1,2:T(8,128)S(1)}) fusion(f32[24,64,4,128]{3,0,1,2:T(8,128)S(1)} %bitcast.173, f32[24,64,4,1]{3,0,1,2:T(8,128)} %copy.253, f32[24,64,4,1]{3,0,1,2:T(8,128)} %copy.256, f32[64,4,129]{2,0,1:T(8,128)S(1)} %get-tuple-element.65), kind=kLoop, calls=%fused_computation | loop fusion | flops 2377728 | bytes 9667584 | tf_op jit(solution)/shard_map/concatenate | solution.py:70
  112.0 1.9 collective-permute-start.9
  113.9 4.3 %collective-permute-start.13 = (f32[24,64,128]{2,0,1:T(8,128)}, f32[24,64,128]{2,0,1:T(8,128)}, u32[]{:S(2)}, u32[]{:S(2)}) collective-permute-start(f32[24,64,128]{2,0,1:T(8,128)} %collective-permute-done.12), channel_id=1, source_target_pairs={{8,0},{16,8},{24,16},{32,24},{40,32},{48,40},{56,48},{9,1},{17,9},... | collective-permute-start | bytes 2359304 | tf_op jit(solution)/shard_map/ppermute | solution.py:56
  118.2 1.9 collective-permute-start.11
  120.2 4.6 %copy_add_fusion = f32[24,64,4,129]{3,0,2,1:T(8,128)} fusion(f32[24,64,4,129]{3,0,1,2:T(8,128)S(1)} %get-tuple-element.53, f32[24,64,4,129]{3,0,1,2:T(8,128)S(1)} %get-tuple-element.52, f32[64,4,129]{2,1,0:T(4,128)} %copy.251), kind=kLoop, calls=%fused_computation.5 | loop fusion | flops 1585152 | bytes 9643008 | tf_op jit(solution)/shard_map/add | solution.py:187
  127.3 25.5 %collective-permute-done.11 = f32[24,64,128]{2,0,1:T(8,128)} collective-permute-done((f32[24,64,128]{2,0,1:T(8,128)}, f32[24,64,128]{2,0,1:T(8,128)}, u32[]{:S(2)}, u32[]{:S(2)}) %collective-permute-start.11) | collective-permute-done | bytes 786464 | tf_op jit(solution)/shard_map/ppermute | solution.py:56
  157.1 6.8 %fusion.7 = f32[24,64,4,128]{3,0,2,1:T(8,128)S(1)} fusion(f32[24,64,4,129]{3,0,2,1:T(8,128)} %copy_add_fusion, f32[24,64,5,128]{3,0,2,1:T(8,128)S(1)} %fusion.1, f32[64,4,128]{2,1,0:T(4,128)} %copy.242, f32[24,64,1,1,4,128]{5,4,3,2,1,0:T(4,128)S(1)} %copy-done.1), kind=kLoop, calls=%fused_computation.20 | loop fusion | flops 3932160 | bytes 19005440 | tf_op jit(solution)/shard_map/mul | solution.py:191
  165.8 8.5 %collective-permute-start.7 = (f32[3,16,16,1]{3,1,2,0:T(8,128)S(1)}, f32[3,16,16,1]{3,1,2,0:T(8,128)S(1)}, u32[]{:S(2)}, u32[]{:S(2)}) collective-permute-start(f32[3,16,16,1]{3,1,2,0:T(8,128)S(1)} %copy-done.25), channel_id=1, source_target_pairs={{0,1},{1,2},{2,3},{3,4},{4,5},{5,6},{6,7},{8,9},{9,10},{10,11},{11... | collective-permute-start | bytes 9224 | tf_op jit(solution)/shard_map/ppermute | solution.py:25
  174.4 4.7 %collective-permute-done.7 = f32[3,16,16,1]{3,1,2,0:T(8,128)S(1)} collective-permute-done((f32[3,16,16,1]{3,1,2,0:T(8,128)S(1)}, f32[3,16,16,1]{3,1,2,0:T(8,128)S(1)}, u32[]{:S(2)}, u32[]{:S(2)}) %collective-permute-start.7) | collective-permute-done | bytes 3104 | tf_op jit(solution)/shard_map/ppermute | solution.py:25
  180.9 2.1 collective-permute-done.17
  183.0 3.4 %collective-permute-start.18 = (f32[24,64,128]{2,0,1:T(8,128)}, f32[24,64,128]{2,0,1:T(8,128)}, u32[]{:S(2)}, u32[]{:S(2)}) collective-permute-start(f32[24,64,128]{2,0,1:T(8,128)} %collective-permute-done.17), channel_id=1, source_target_pairs={{0,8},{8,16},{16,24},{24,32},{32,40},{40,48},{48,56},{1,9},{9,17},... | collective-permute-start | bytes 2359304 | tf_op jit(solution)/shard_map/ppermute | solution.py:56
  186.4 3.8 %fusion.71 = (f32[24,64,4,1]{3,0,2,1:T(8,128)}, f32[24,64,4,1]{3,0,2,1:T(8,128)}) fusion(f32[24,64,4,128]{3,0,2,1:T(8,128)S(1)} %fusion.7), kind=kLoop, calls=%fused_computation.161 | loop fusion | bytes 98304 | tf_op jit(solution)/shard_map/slice | solution.py:68
  190.2 3.3 %copy.263 = f32[24,64,4,1]{1,0,3,2:T(8,128)} copy(f32[24,64,4,1]{3,0,2,1:T(8,128)} %get-tuple-element.49) | data formatting | bytes 49152 | tf_op jit(solution)/shard_map/slice | solution.py:69
  193.5 8.3 %collective-permute-start.21 = (f32[24,64,4,1]{1,0,3,2:T(8,128)}, f32[24,64,4,1]{1,0,3,2:T(8,128)}, u32[]{:S(2)}, u32[]{:S(2)}) collective-permute-start(f32[24,64,4,1]{1,0,3,2:T(8,128)} %copy.263), channel_id=1, source_target_pairs={{0,1},{1,2},{2,3},{3,4},{4,5},{5,6},{6,7},{8,9},{9,10},{10,11},{11... | collective-permute-start | bytes 73736 | tf_op jit(solution)/shard_map/ppermute | solution.py:72
  201.8 3.2 %copy.265 = f32[24,64,4,1]{1,0,3,2:T(8,128)} copy(f32[24,64,4,1]{3,0,2,1:T(8,128)} %get-tuple-element.48) | data formatting | bytes 49152 | tf_op jit(solution)/shard_map/slice | solution.py:68
  205.0 1.9 collective-permute-start.22
  207.0 4.8 %collective-permute-start.20 = (f32[24,64,128]{2,0,1:T(8,128)}, f32[24,64,128]{2,0,1:T(8,128)}, u32[]{:S(2)}, u32[]{:S(2)}) collective-permute-start(f32[24,64,128]{2,0,1:T(8,128)} %collective-permute-done.19), channel_id=1, source_target_pairs={{8,0},{16,8},{24,16},{32,24},{40,32},{48,40},{56,48},{9,1},{17,9},... | collective-permute-start | bytes 2359304 | tf_op jit(solution)/shard_map/ppermute | solution.py:56
  216.5 3.2 %copy.264 = f32[24,64,4,1]{3,0,2,1:T(8,128)} copy(f32[24,64,4,1]{1,0,3,2:T(8,128)} %collective-permute-done.21) | data formatting | bytes 49152 | tf_op jit(solution)/shard_map/ppermute | solution.py:72
  219.7 3.2 %copy.266 = f32[24,64,4,1]{3,0,2,1:T(8,128)} copy(f32[24,64,4,1]{1,0,3,2:T(8,128)} %collective-permute-done.22) | data formatting | bytes 49152 | tf_op jit(solution)/shard_map/ppermute | solution.py:74
  222.9 4.3 %fusion = f32[24,64,4,129]{3,0,2,1:T(8,128)S(1)} fusion(f32[24,64,4,128]{3,0,2,1:T(8,128)S(1)} %fusion.7, f32[24,64,4,1]{3,0,2,1:T(8,128)} %copy.264, f32[24,64,4,1]{3,0,2,1:T(8,128)} %copy.266, f32[64,4,129]{2,1,0:T(4,128)} %copy.288, f32[64,4,129]{2,1,0:T(4,128)S(1)} %copy-done.8), kind=kLoop, calls=%fused_computation.3 | loop fusion | flops 3962880 | bytes 6629376 | tf_op jit(solution)/shard_map/add | solution.py:187
  234.0 1.7 fusion.67
  236.7 4.8 %all-to-all-start.3 = ((f32[64,4,128]{2,1,0:T(4,128)}), f32[64,4,128]{2,1,0:T(4,128)S(1)}, u32[]{:S(2)}, u32[]{:S(2)}) async-start(f32[64,4,128]{2,1,0:T(4,128)} %copy.271), calls=%async_computation.3 | async-start | bytes 262144 | tf_op jit(solution)/shard_map/all_to_all | solution.py:207
  241.7 7.0 %fusion.9 = f32[24,64,1,1,4,128]{5,0,4,1,3,2:T(8,128)S(1)} fusion(f32[24,64,4,128]{3,0,2,1:T(8,128)} %copy-done.2, f32[24]{0:T(128)} %param.24, f32[64,4,128]{2,1,0:T(4,128)S(1)} %copy.275, f32[24]{0:T(128)} %param.23, f32[64,4,128]{2,1,0:T(4,128)S(1)} %bitcast.188, f32[24]{0:T(128)} %param.22, f32[64,4,128]{2,1,0:T(4,128)S(1)} %copy.274, ...), kind=kOutput, calls=%fused_computation.24 | convolution fusion | flops 233570304 | bytes 6687264 | tf_op jit(solution)/shard_map/dot_general | solution.py:215
  248.7 2.5 copy.281
  (161 shorter events, 51.5 us)
Async XLA Ops:
  0.6 241.0 %copy-start = (f32[24,24]{1,0:T(8,128)S(1)}, f32[24,24]{1,0:T(8,128)}, u32[]{:S(2)}) copy-start(f32[24,24]{1,0:T(8,128)} %param.25) | copy-start | bytes 6916
  1.5 32.5 %collective-permute-start.3 = (s32[2,16,1]{2,1,0:T(8,128)S(1)}, s32[2,16,1]{2,1,0:T(8,128)S(1)}, u32[]{:S(2)}, u32[]{:S(2)}) collective-permute-start(s32[2,16,1]{2,1,0:T(8,128)S(1)} %get-tuple-element.77), channel_id=1, source_target_pairs={{1,0},{2,1},{3,2},{4,3},{5,4},{6,5},{7,6},{9,8},{10,9},{11,10},{12... | collective-permute-start | bytes 392 | tf_op jit(solution)/shard_map/ppermute | solution.py:26
  4.1 32.1 %collective-permute-start = (s32[2,16,1]{2,1,0:T(8,128)S(1)}, s32[2,16,1]{2,1,0:T(8,128)S(1)}, u32[]{:S(2)}, u32[]{:S(2)}) collective-permute-start(s32[2,16,1]{2,1,0:T(8,128)S(1)} %get-tuple-element.76), channel_id=1, source_target_pairs={{0,1},{1,2},{2,3},{3,4},{4,5},{5,6},{6,7},{8,9},{9,10},{10,11},{11... | collective-permute-start | bytes 392 | tf_op jit(solution)/shard_map/ppermute | solution.py:25
  9.6 26.6 %collective-permute-start.2 = (s32[2,1,128]{2,1,0:T(1,128)S(1)}, s32[2,1,128]{2,1,0:T(1,128)S(1)}, u32[]{:S(2)}, u32[]{:S(2)}) collective-permute-start(s32[2,1,128]{2,1,0:T(1,128)S(1)} %get-tuple-element.75), channel_id=1, source_target_pairs={{8,0},{16,8},{24,16},{32,24},{40,32},{48,40},{56,48},{9,1},{17,9},... | collective-permute-start | bytes 3080 | tf_op jit(solution)/shard_map/ppermute | solution.py:26
  13.4 22.8 %collective-permute-start.1 = (s32[2,1,128]{2,1,0:T(1,128)S(1)}, s32[2,1,128]{2,1,0:T(1,128)S(1)}, u32[]{:S(2)}, u32[]{:S(2)}) collective-permute-start(s32[2,1,128]{2,1,0:T(1,128)S(1)} %get-tuple-element.74), channel_id=1, source_target_pairs={{0,8},{8,16},{16,24},{24,32},{32,40},{40,48},{48,56},{1,9},{9,17},... | collective-permute-start | bytes 3080 | tf_op jit(solution)/shard_map/ppermute | solution.py:25
  22.7 7.6 %copy-start.32 = (s32[16,128]{1,0:T(8,128)S(1)}, s32[16,128]{1,0:T(8,128)}, u32[]{:S(2)}) copy-start(s32[16,128]{1,0:T(8,128)} %param.18) | copy-start | bytes 24580
  22.7 7.6 %copy-start.31 = (s32[16,128]{1,0:T(8,128)S(1)}, s32[16,128]{1,0:T(8,128)}, u32[]{:S(2)}) copy-start(s32[16,128]{1,0:T(8,128)} %param.17) | copy-start | bytes 24580
  25.9 58.8 %collective-permute-start.15 = (f32[24,64,4,1]{1,0,3,2:T(8,128)}, f32[24,64,4,1]{1,0,3,2:T(8,128)}, u32[]{:S(2)}, u32[]{:S(2)}) collective-permute-start(f32[24,64,4,1]{1,0,3,2:T(8,128)} %copy.252), channel_id=1, source_target_pairs={{0,1},{1,2},{2,3},{3,4},{4,5},{5,6},{6,7},{8,9},{9,10},{10,11},{11... | collective-permute-start | bytes 73736 | tf_op jit(solution)/shard_map/ppermute | solution.py:72
  28.5 8.7 %copy-start.30 = (f32[16,16,128]{2,1,0:T(8,128)S(1)}, f32[16,16,128]{2,1,0:T(8,128)}, u32[]{:S(2)}) copy-start(f32[16,16,128]{2,1,0:T(8,128)} %param.16) | copy-start | bytes 393220
  34.0 53.6 %collective-permute-start.16 = (f32[24,64,4,1]{1,0,3,2:T(8,128)}, f32[24,64,4,1]{1,0,3,2:T(8,128)}, u32[]{:S(2)}, u32[]{:S(2)}) collective-permute-start(f32[24,64,4,1]{1,0,3,2:T(8,128)} %copy.255), channel_id=1, source_target_pairs={{1,0},{2,1},{3,2},{4,3},{5,4},{6,5},{7,6},{9,8},{10,9},{11,10},{12... | collective-permute-start | bytes 73736 | tf_op jit(solution)/shard_map/ppermute | solution.py:74
  39.5 7.5 %all-to-all-start = ((f32[4,1,16,128]{3,2,1,0:T(8,128)}), f32[4,1,16,128]{3,2,1,0:T(8,128)S(1)}, u32[]{:S(2)}, u32[]{:S(2)}) async-start(f32[4,1,16,128]{3,2,1,0:T(8,128)} %broadcast_in_dim.10), calls=%async_computation | async-start | bytes 65536 | tf_op jit(solution)/shard_map/all_to_all | solution.py:39
  47.0 11.9 %copy-start.5 = (f32[16,18,130]{2,0,1:T(8,128)S(1)}, f32[16,18,130]{2,0,1:T(8,128)}, u32[]{:S(2)}) copy-start(f32[16,18,130]{2,0,1:T(8,128)} %copy-done.4) | copy-start | bytes 449284
  47.0 20.7 %copy-start.12 = (f32[16,16,129]{2,0,1:T(8,128)S(1)}, f32[16,16,129]{2,0,1:T(8,128)}, u32[]{:S(2)}) copy-start(f32[16,16,129]{2,0,1:T(8,128)} %slice_multiply_fusion) | copy-start | bytes 396292
  50.0 15.1 %collective-permute-start.6 = (f32[3,16,16,1]{3,1,2,0:T(8,128)S(1)}, f32[3,16,16,1]{3,1,2,0:T(8,128)S(1)}, u32[]{:S(2)}, u32[]{:S(2)}) collective-permute-start(f32[3,16,16,1]{3,1,2,0:T(8,128)S(1)} %get-tuple-element.57), channel_id=1, source_target_pairs={{1,0},{2,1},{3,2},{4,3},{5,4},{6,5},{7,6},{9,8},{10,9},{11,10},{12... | collective-permute-start | bytes 9224 | tf_op jit(solution)/shard_map/ppermute | solution.py:26
  52.7 14.0 %collective-permute-start.4 = (f32[3,16,1,128]{3,1,2,0:T(8,128)S(1)}, f32[3,16,1,128]{3,1,2,0:T(8,128)S(1)}, u32[]{:S(2)}, u32[]{:S(2)}) collective-permute-start(f32[3,16,1,128]{3,1,2,0:T(8,128)S(1)} %get-tuple-element.61), channel_id=1, source_target_pairs={{8,0},{16,8},{24,16},{32,24},{40,32},{48,40},{56,48},{9,1},{17,9},... | collective-permute-start | bytes 73736 | tf_op jit(solution)/shard_map/ppermute | solution.py:26
  57.0 9.7 %collective-permute-start.5 = (f32[3,16,1,128]{3,1,2,0:T(8,128)S(1)}, f32[3,16,1,128]{3,1,2,0:T(8,128)S(1)}, u32[]{:S(2)}, u32[]{:S(2)}) collective-permute-start(f32[3,16,1,128]{3,1,2,0:T(8,128)S(1)} %get-tuple-element.60), channel_id=1, source_target_pairs={{0,8},{8,16},{16,24},{24,32},{32,40},{40,48},{48,56},{1,9},{9,17},... | collective-permute-start | bytes 73736 | tf_op jit(solution)/shard_map/ppermute | solution.py:25
  59.1 10.5 %copy-start.18 = (f32[16,17,128]{2,0,1:T(8,128)}, f32[16,17,128]{2,0,1:T(8,128)S(1)}, u32[]{:S(2)}) copy-start(f32[16,17,128]{2,0,1:T(8,128)S(1)} %slice_multiply_fusion.1) | copy-start | bytes 417796
  65.1 48.8 %collective-permute-start.12 = (f32[24,64,128]{2,0,1:T(8,128)}, f32[24,64,128]{2,0,1:T(8,128)}, u32[]{:S(2)}, u32[]{:S(2)}) collective-permute-start(f32[24,64,128]{2,0,1:T(8,128)} %get-tuple-element.51), channel_id=1, source_target_pairs={{0,192},{64,0},{128,64},{192,128},{1,193},{65,1},{129,65},{193,129... | collective-permute-start | bytes 2359304 | tf_op jit(solution)/shard_map/ppermute | solution.py:61
  66.7 3.5 %copy-start.26 = (f32[3,16,1,128]{3,1,2,0:T(8,128)}, f32[3,16,1,128]{3,1,2,0:T(8,128)S(1)}, u32[]{:S(2)}) copy-start(f32[3,16,1,128]{3,1,2,0:T(8,128)S(1)} %collective-permute-done.4) | copy-start | bytes 73732
  66.7 51.5 %collective-permute-start.10 = (f32[24,64,128]{2,0,1:T(8,128)}, f32[24,64,128]{2,0,1:T(8,128)}, u32[]{:S(2)}, u32[]{:S(2)}) collective-permute-start(f32[24,64,128]{2,0,1:T(8,128)} %get-tuple-element.50), channel_id=1, source_target_pairs={{0,64},{64,128},{128,192},{192,0},{1,65},{65,129},{129,193},{193,1... | collective-permute-start | bytes 2359304 | tf_op jit(solution)/shard_map/ppermute | solution.py:61
  66.7 3.5 %copy-start.28 = (f32[3,16,1,128]{3,1,2,0:T(8,128)}, f32[3,16,1,128]{3,1,2,0:T(8,128)S(1)}, u32[]{:S(2)}) copy-start(f32[3,16,1,128]{3,1,2,0:T(8,128)S(1)} %collective-permute-done.5) | copy-start | bytes 73732
  70.9 19.7 %all-to-all-start.2 = ((f32[4,16,4,128]{3,1,2,0:T(8,128)}), f32[4,16,4,128]{3,1,2,0:T(8,128)}, u32[]{:S(2)}, u32[]{:S(2)}) async-start(f32[4,16,4,128]{3,1,2,0:T(8,128)} %pad_maximum_fusion.14), calls=%async_computation.2 | async-start | bytes 262144 | tf_op jit(solution)/shard_map/all_to_all | solution.py:140
  90.6 9.9 %all-to-all-start.1 = ((f32[16,16,128]{2,0,1:T(8,128)}), f32[16,16,128]{2,0,1:T(8,128)}, u32[]{:S(2)}, u32[]{:S(2)}) async-start(f32[16,16,128]{2,0,1:T(8,128)} %get-tuple-element.59), calls=%async_computation.1 | async-start | bytes 262144 | tf_op jit(solution)/shard_map/all_to_all | solution.py:138
  97.2 6.7 %collective-permute-start.14 = (f32[64,4]{0,1:T(4,128)}, f32[64,4]{0,1:T(4,128)}, u32[]{:S(2)}, u32[]{:S(2)}) collective-permute-start(f32[64,4]{0,1:T(4,128)} %slice_reduce_fusion), channel_id=1, source_target_pairs={{0,1},{1,2},{2,3},{3,4},{4,5},{5,6},{6,7},{8,9},{9,10},{10,11},{11... | collective-permute-start | bytes 3080 | tf_op jit(solution)/shard_map/ppermute | solution.py:56
  102.7 9.3 %collective-permute-start.8 = (f32[64,128]{1,0:T(8,128)}, f32[64,128]{1,0:T(8,128)}, u32[]{:S(2)}, u32[]{:S(2)}) collective-permute-start(f32[64,128]{1,0:T(8,128)} %slice_bitcast_fusion.11), channel_id=1, source_target_pairs={{0,64},{64,128},{128,192},{192,0},{1,65},{65,129},{129,193},{193,1... | collective-permute-start | bytes 98312 | tf_op jit(solution)/shard_map/ppermute | solution.py:61
  106.4 4.7 %copy-start.9 = (f32[64,4,129]{2,0,1:T(8,128)}, f32[64,4,129]{2,0,1:T(8,128)S(1)}, u32[]{:S(2)}) copy-start(f32[64,4,129]{2,0,1:T(8,128)S(1)} %get-tuple-element.65) | copy-start | bytes 396292
  112.0 12.7 %collective-permute-start.9 = (f32[64,128]{1,0:T(8,128)}, f32[64,128]{1,0:T(8,128)S(1)}, u32[]{:S(2)}, u32[]{:S(2)}) collective-permute-start(f32[64,128]{1,0:T(8,128)} %collective-permute-done.8), channel_id=1, source_target_pairs={{0,8},{8,16},{16,24},{24,32},{32,40},{40,48},{48,56},{1,9},{9,17},... | collective-permute-start | bytes 98312 | tf_op jit(solution)/shard_map/ppermute | solution.py:56
  113.9 40.0 %collective-permute-start.13 = (f32[24,64,128]{2,0,1:T(8,128)}, f32[24,64,128]{2,0,1:T(8,128)}, u32[]{:S(2)}, u32[]{:S(2)}) collective-permute-start(f32[24,64,128]{2,0,1:T(8,128)} %collective-permute-done.12), channel_id=1, source_target_pairs={{8,0},{16,8},{24,16},{32,24},{40,32},{48,40},{56,48},{9,1},{17,9},... | collective-permute-start | bytes 2359304 | tf_op jit(solution)/shard_map/ppermute | solution.py:56
  118.2 34.5 %collective-permute-start.11 = (f32[24,64,128]{2,0,1:T(8,128)}, f32[24,64,128]{2,0,1:T(8,128)}, u32[]{:S(2)}, u32[]{:S(2)}) collective-permute-start(f32[24,64,128]{2,0,1:T(8,128)} %collective-permute-done.10), channel_id=1, source_target_pairs={{0,8},{8,16},{16,24},{24,32},{32,40},{40,48},{48,56},{1,9},{9,17},... | collective-permute-start | bytes 2359304 | tf_op jit(solution)/shard_map/ppermute | solution.py:56
  124.7 30.5 %copy-start.3 = (f32[24,64,1,1,4,128]{5,0,4,1,2,3:T(8,128)S(1)}, f32[24,64,1,1,4,128]{5,0,4,1,2,3:T(8,128)}, u32[]{:S(2)}) copy-start(f32[24,64,1,1,4,128]{5,0,4,1,2,3:T(8,128)} %copy.346) | copy-start | bytes 9437188
  126.6 28.6 %copy-start.16 = (f32[64,5,128]{2,0,1:T(8,128)}, f32[64,5,128]{2,0,1:T(8,128)S(1)}, u32[]{:S(2)}) copy-start(f32[64,5,128]{2,0,1:T(8,128)S(1)} %get-tuple-element.67) | copy-start | bytes 491524
  163.9 15.2 %copy-start.7 = (f32[3,16,18,129]{3,1,2,0:T(8,128)S(1)}, f32[3,16,18,129]{3,1,2,0:T(8,128)}, u32[]{:S(2)}) copy-start(f32[3,16,18,129]{3,1,2,0:T(8,128)} %copy-done.6) | copy-start | bytes 1337476
  163.9 15.2 %copy-start.13 = (f32[16,16,129]{2,0,1:T(8,128)S(1)}, f32[16,16,129]{2,0,1:T(8,128)}, u32[]{:S(2)}) copy-start(f32[16,16,129]{2,0,1:T(8,128)} %slice_multiply_fusion) | copy-start | bytes 396292
  163.9 15.2 %copy-start.27 = (f32[3,16,1,128]{3,1,2,0:T(8,128)S(1)}, f32[3,16,1,128]{3,1,2,0:T(8,128)}, u32[]{:S(2)}) copy-start(f32[3,16,1,128]{3,1,2,0:T(8,128)} %copy-done.26) | copy-start | bytes 73732
  163.9 15.2 %copy-start.29 = (f32[3,16,1,128]{3,1,2,0:T(8,128)S(1)}, f32[3,16,1,128]{3,1,2,0:T(8,128)}, u32[]{:S(2)}) copy-start(f32[3,16,1,128]{3,1,2,0:T(8,128)} %copy-done.28) | copy-start | bytes 73732
  163.9 16.1 %copy-start.19 = (f32[16,17,128]{2,0,1:T(8,128)S(1)}, f32[16,17,128]{2,0,1:T(8,128)}, u32[]{:S(2)}) copy-start(f32[16,17,128]{2,0,1:T(8,128)} %copy-done.18) | copy-start | bytes 417796
  164.9 18.1 %collective-permute-start.17 = (f32[24,64,128]{2,0,1:T(8,128)S(1)}, f32[24,64,128]{2,0,1:T(8,128)}, u32[]{:S(2)}, u32[]{:S(2)}) collective-permute-start(f32[24,64,128]{2,0,1:T(8,128)S(1)} %get-tuple-element.47), channel_id=1, source_target_pairs={{0,64},{64,128},{128,192},{192,0},{1,65},{65,129},{129,193},{193,1... | collective-permute-start | bytes 2359304 | tf_op jit(solution)/shard_map/ppermute | solution.py:61
  165.8 13.3 %collective-permute-start.7 = (f32[3,16,16,1]{3,1,2,0:T(8,128)S(1)}, f32[3,16,16,1]{3,1,2,0:T(8,128)S(1)}, u32[]{:S(2)}, u32[]{:S(2)}) collective-permute-start(f32[3,16,16,1]{3,1,2,0:T(8,128)S(1)} %copy-done.25), channel_id=1, source_target_pairs={{0,1},{1,2},{2,3},{3,4},{4,5},{5,6},{6,7},{8,9},{9,10},{10,11},{11... | collective-permute-start | bytes 9224 | tf_op jit(solution)/shard_map/ppermute | solution.py:25
  179.4 27.6 %collective-permute-start.19 = (f32[24,64,128]{2,0,1:T(8,128)}, f32[24,64,128]{2,0,1:T(8,128)}, u32[]{:S(2)}, u32[]{:S(2)}) collective-permute-start(f32[24,64,128]{2,0,1:T(8,128)} %get-tuple-element.46), channel_id=1, source_target_pairs={{0,192},{64,0},{128,64},{192,128},{1,193},{65,1},{129,65},{193,129... | collective-permute-start | bytes 2359304 | tf_op jit(solution)/shard_map/ppermute | solution.py:61
  183.0 44.2 %collective-permute-start.18 = (f32[24,64,128]{2,0,1:T(8,128)}, f32[24,64,128]{2,0,1:T(8,128)}, u32[]{:S(2)}, u32[]{:S(2)}) collective-permute-start(f32[24,64,128]{2,0,1:T(8,128)} %collective-permute-done.17), channel_id=1, source_target_pairs={{0,8},{8,16},{16,24},{24,32},{32,40},{40,48},{48,56},{1,9},{9,17},... | collective-permute-start | bytes 2359304 | tf_op jit(solution)/shard_map/ppermute | solution.py:56
  190.2 24.1 %copy-start.22 = (f32[16,16,128]{2,0,1:T(8,128)S(1)}, f32[16,16,128]{2,0,1:T(8,128)}, u32[]{:S(2)}) copy-start(f32[16,16,128]{2,0,1:T(8,128)} %copy-done.21) | copy-start | bytes 393220
  190.2 25.4 %copy-start.10 = (f32[64,4,129]{2,0,1:T(8,128)S(1)}, f32[64,4,129]{2,0,1:T(8,128)}, u32[]{:S(2)}) copy-start(f32[64,4,129]{2,0,1:T(8,128)} %copy-done.9) | copy-start | bytes 396292
  193.5 23.0 %collective-permute-start.21 = (f32[24,64,4,1]{1,0,3,2:T(8,128)}, f32[24,64,4,1]{1,0,3,2:T(8,128)}, u32[]{:S(2)}, u32[]{:S(2)}) collective-permute-start(f32[24,64,4,1]{1,0,3,2:T(8,128)} %copy.263), channel_id=1, source_target_pairs={{0,1},{1,2},{2,3},{3,4},{4,5},{5,6},{6,7},{8,9},{9,10},{10,11},{11... | collective-permute-start | bytes 73736 | tf_op jit(solution)/shard_map/ppermute | solution.py:72
  205.0 14.7 %collective-permute-start.22 = (f32[24,64,4,1]{1,0,3,2:T(8,128)}, f32[24,64,4,1]{1,0,3,2:T(8,128)}, u32[]{:S(2)}, u32[]{:S(2)}) collective-permute-start(f32[24,64,4,1]{1,0,3,2:T(8,128)} %copy.265), channel_id=1, source_target_pairs={{1,0},{2,1},{3,2},{4,3},{5,4},{6,5},{7,6},{9,8},{10,9},{11,10},{12... | collective-permute-start | bytes 73736 | tf_op jit(solution)/shard_map/ppermute | solution.py:74
  207.0 21.6 %collective-permute-start.20 = (f32[24,64,128]{2,0,1:T(8,128)}, f32[24,64,128]{2,0,1:T(8,128)}, u32[]{:S(2)}, u32[]{:S(2)}) collective-permute-start(f32[24,64,128]{2,0,1:T(8,128)} %collective-permute-done.19), channel_id=1, source_target_pairs={{8,0},{16,8},{24,16},{32,24},{40,32},{48,40},{56,48},{9,1},{17,9},... | collective-permute-start | bytes 2359304 | tf_op jit(solution)/shard_map/ppermute | solution.py:56
  216.5 6.4 %copy-start.8 = (f32[64,4,129]{2,1,0:T(4,128)S(1)}, f32[64,4,129]{2,1,0:T(4,128)}, u32[]{:S(2)}) copy-start(f32[64,4,129]{2,1,0:T(4,128)} %copy.251) | copy-start | bytes 396292
  232.3 3.4 %copy-start.33 = (pred[4,128]{1,0:T(4,128)(4,1)S(1)}, pred[4,128]{1,0:T(4,128)(4,1)}, u32[]{:S(2)}) copy-start(pred[4,128]{1,0:T(4,128)(4,1)} %dynamic-slice_compare_fusion) | copy-start | bytes 1540
  236.7 14.5 %all-to-all-start.3 = ((f32[64,4,128]{2,1,0:T(4,128)}), f32[64,4,128]{2,1,0:T(4,128)S(1)}, u32[]{:S(2)}, u32[]{:S(2)}) async-start(f32[64,4,128]{2,1,0:T(4,128)} %copy.271), calls=%async_computation.3 | async-start | bytes 262144 | tf_op jit(solution)/shard_map/all_to_all | solution.py:207
  (15 other events, 24.9 us)
